TPU v7x, 128 devices: a whole 4x4x4 slice. The times are simulated.
128 devices in a mesh: tm: 16 (over x_hi, y, core), height: 8 (over x_lo, z).
Axes of the slice: x: 4 (x_hi: 2, x_lo: 2; x = x_hi * 2 + x_lo), y: 4, z: 4, core: 2. Of those that a mesh axis runs over, the one named last changes fastest.
Arguments:
- tokens: bfloat16 [32, 32, 80, 3072], P('tm', 'height'), may hold values from -6 to 6
- mod_scale: float32 [3072], replicated, may hold values from -3 to 3
- mod_shift: float32 [3072], replicated, may hold values from -3 to 3
- w_qkv: bfloat16 [3072, 4608], P(('tm', 'height')), may hold values from -0.109375 to 0.109375
- q_gain: float32 [128], replicated, may hold values from 0.25 to 1.75
- k_gain: float32 [128], replicated, may hold values from 0.25 to 1.75
- window: int32 [12, 3], replicated, may hold values from 0 to 2, as said below
- valid: int32 [32, 32, 80], replicated, may hold values from 0 to 1, as said below
Outputs:
- attended: bfloat16 [32, 32, 80, 1536], P('tm', 'height')
Inputs may be any that keep to these rules, and one draw needn't show every extreme that they name: `window`: column 0 is at most 1, column 1 at most 1, column 2 at most 2; some head has all three at these most values. `valid`: the last frames, rows and columns of the grid may be padding with 0; scattered tokens elsewhere are 0 too.
All inputs are finite; a program needn't handle non-finite values.
Results may differ from a plain program's by a relative error of at most 0.0055.
Values may be sent and summed in bfloat16 or wider, within the bound.
A program may use at most 128 MiB of HBM per device.

v0:
```python
import jax
import jax.numpy as jnp
from jax import lax
from jax.sharding import PartitionSpec as P

HDIM = 128
HEADS = 12
TT = 1
TH = 2
TW = 8
EPS = 1e-06


def with_halo(cells, sides, width):
    for axis, dim in sides:
        count = lax.axis_size(axis)
        ends = count - 1
        head = lax.slice_in_dim(cells, 0, width, axis=dim)
        tail = lax.slice_in_dim(cells, cells.shape[dim] - width, cells.shape[dim], axis=dim)
        cells = jnp.concatenate(
            [
                lax.ppermute(tail, axis, [(i, (i + 1) % count) for i in range(ends)]),
                cells,
                lax.ppermute(head, axis, [((i + 1) % count, i) for i in range(ends)]),
            ],
            axis=dim,
        )
    return cells


def modulate(tokens, mod_scale, mod_shift):
    values = tokens.astype(jnp.float32)
    mean = jnp.mean(values, axis=-1, keepdims=True)
    centred = values - mean
    variance = jnp.mean(centred * centred, axis=-1, keepdims=True)
    normed = centred * lax.rsqrt(variance + EPS)
    return (normed * (1.0 + mod_scale) + mod_shift).astype(jnp.bfloat16)


def head_norm(values, gain):
    power = jnp.mean(values * values, axis=-1, keepdims=True)
    return (values * lax.rsqrt(power + EPS) * gain).astype(jnp.bfloat16)


def tile_coords(frames, rows, width):
    shape = (frames.shape[0], rows.shape[0], width)
    columns = jnp.arange(width, dtype=jnp.int32)
    frame_tiles = jnp.broadcast_to((frames // TT)[:, None, None], shape).reshape(-1)
    row_tiles = jnp.broadcast_to((rows // TH)[None, :, None], shape).reshape(-1)
    column_tiles = jnp.broadcast_to((columns // TW)[None, None, :], shape).reshape(-1)
    return (frame_tiles, row_tiles, column_tiles)


def per_device(tokens, mod_scale, mod_shift, w_qkv, q_gain, k_gain, window, valid):
    frame_count, row_count, width, features = tokens.shape
    token_count = frame_count * row_count * width
    modulated = modulate(tokens.reshape(token_count, features), mod_scale, mod_shift)
    full_weight = lax.all_gather(w_qkv, ("tm", "height"), axis=0, tiled=True)
    qkv = jnp.dot(modulated, full_weight, preferred_element_type=jnp.float32)
    inner = qkv.shape[1] // 3
    query = head_norm(qkv[:, :inner].reshape(token_count, HEADS, HDIM), q_gain)
    key = head_norm(qkv[:, inner : 2 * inner].reshape(token_count, HEADS, HDIM), k_gain)
    value = qkv[:, 2 * inner :].astype(jnp.bfloat16)
    tiled = (frame_count // TT, TT, row_count // TH, TH, width, inner)
    stacked = jnp.stack([key.reshape(tiled), value.reshape(tiled)])
    extended = with_halo(stacked, (("tm", 1), ("height", 3)), 1)
    frames_ext = frame_count + 2 * TT
    rows_ext = row_count + 2 * TH
    key_count = frames_ext * rows_ext * width
    extended = extended.reshape(2, key_count, HEADS, HDIM)
    key_heads = jnp.transpose(extended[0], (1, 0, 2))
    value_heads = jnp.transpose(extended[1], (1, 0, 2))
    query_heads = jnp.transpose(query, (1, 0, 2))
    frame_block = lax.axis_index("tm")
    row_block = lax.axis_index("height")
    first_frame = frame_block * frame_count
    first_row = row_block * row_count
    zero = jnp.int32(0)
    valid_pad = jnp.pad(valid, ((TT, TT), (TH, TH), (0, 0)))
    key_valid = (
        lax.dynamic_slice(
            valid_pad, (first_frame, first_row, zero), (frames_ext, rows_ext, width)
        ).reshape(-1)
        > 0
    )
    query_valid = (
        lax.dynamic_slice(
            valid, (first_frame, first_row, zero), (frame_count, row_count, width)
        ).reshape(-1)
        > 0
    )
    query_coords = tile_coords(
        first_frame + jnp.arange(frame_count, dtype=jnp.int32),
        first_row + jnp.arange(row_count, dtype=jnp.int32),
        width,
    )
    key_coords = tile_coords(
        first_frame - TT + jnp.arange(frames_ext, dtype=jnp.int32),
        first_row - TH + jnp.arange(rows_ext, dtype=jnp.int32),
        width,
    )
    apart_t, apart_h, apart_w = (
        jnp.abs(qa[:, None] - ka[None, :]) for qa, ka in zip(query_coords, key_coords)
    )
    seen = key_valid[None, :]
    scale = 1.0 / jnp.sqrt(jnp.float32(HDIM))

    def per_head(inputs):
        query_one, key_one, value_one, reach = inputs
        allowed = (apart_t <= reach[0]) & (apart_h <= reach[1]) & (apart_w <= reach[2]) & seen
        scores = (
            jnp.einsum("qd,kd->qk", query_one, key_one, preferred_element_type=jnp.float32) * scale
        )
        terms = jnp.where(allowed, jnp.exp(scores), jnp.float32(0.0))
        total = jnp.sum(terms, axis=-1, keepdims=True)
        total = jnp.where(query_valid[:, None], total, jnp.float32(1.0))
        weights = (terms / total).astype(jnp.bfloat16)
        result = jnp.dot(weights, value_one, preferred_element_type=jnp.float32)
        return jnp.where(query_valid[:, None], result, jnp.float32(0.0)).astype(jnp.bfloat16)

    heads_out = lax.map(per_head, (query_heads, key_heads, value_heads, window))
    attended = jnp.transpose(heads_out, (1, 0, 2)).reshape(frame_count, row_count, width, inner)
    return attended


def solution(mesh):
    in_specs = (
        P("tm", "height", None, None),
        P(),
        P(),
        P(("tm", "height"), None),
        P(),
        P(),
        P(),
        P(),
    )
    out_specs = P("tm", "height", None, None)
    return jax.shard_map(
        per_device, mesh=mesh, in_specs=in_specs, out_specs=out_specs, check_vma=False
    )
```

profile of v0, /device:TPU:4, one launch (start us, length us, event | category | flops | bytes accessed | tf_op | source)
XLA Modules:
  0.0 750.8 jit_solution(9672114326475516388)
XLA Ops:
  18.4 334.2 %all-gather.2.cloned.1.call-done = bf16[3072,4608]{1,0:T(8,128)(2,1)} async-done(((bf16[24,4608]{1,0:T(8,128)(2,1)}), bf16[3072,4608]{1,0:T(8,128)(2,1)}) %all-gather.2.cloned.1.call-update) | async-done | bytes 28311568 | tf_op jit(solution)/shard_map/all_gather | solution.py:58
  352.6 23.6 %fusion.33 = f32[640,4608]{1,0:T(8,128)S(1)} fusion(bf16[640,3072]{1,0:T(8,128)(2,1)} %fusion.25, bf16[3072,4608]{1,0:T(8,128)(2,1)} %all-gather.2.cloned.1.call-done), kind=kOutput, calls=%fused_computation.72 | convolution fusion | flops 18119393280 | bytes 44040192 | tf_op jit(solution)/shard_map/dot_general | solution.py:59
  406.8 6.3 collective-permute-start.1
  413.1 20.4 %collective-permute-done = bf16[2,1,1,2,2,80,1536]{6,5,4,3,1,2,0:T(8,128)(2,1)S(1)} collective-permute-done((bf16[2,1,1,2,2,80,1536]{6,5,4,3,1,2,0:T(8,128)(2,1)S(1)}, bf16[2,1,1,2,2,80,1536]{6,5,4,3,1,2,0:T(8,128)(2,1)S(1)}, u32[]{:S(2)}, u32[]{:S(2)}) %collective-permute-start) | collective-permute-done | bytes 1966112 | tf_op jit(solution)/shard_map/ppermute | solution.py:22
  460.1 67.4 %collective-permute-done.2 = bf16[2,4,1,1,2,80,1536]{6,5,4,3,1,2,0:T(8,128)(2,1)} collective-permute-done((bf16[2,4,1,1,2,80,1536]{6,5,4,3,1,2,0:T(8,128)(2,1)}, bf16[2,4,1,1,2,80,1536]{6,5,4,3,1,2,0:T(8,128)(2,1)}, u32[]{:S(2)}, u32[]{:S(2)}) %collective-permute-start.2) | collective-permute-done | bytes 3932192 | tf_op jit(solution)/shard_map/ppermute | solution.py:22
  527.5 6.0 collective-permute-done.3
  533.4 6.5 pad_maximum_fusion
  545.7 15.1 %squeeze.28 = bf16[2560,12,128]{2,1,0:T(8,128)(2,1)} reshape(bf16[1,4,1,4,2,80,1536]{6,5,4,3,1,2,0:T(8,128)(2,1)} %get-tuple-element.149) | data formatting | bytes 15728640 | tf_op jit(solution)/shard_map/squeeze | solution.py:71
  560.8 9.2 %copy.16 = bf16[12,2560,128]{2,1,0:T(8,128)(2,1)} copy(bf16[12,2560,128]{2,0,1:T(8,128)(2,1)} %bitcast.66) | data formatting | bytes 15728640
  570.0 15.1 %squeeze.29 = bf16[2560,12,128]{2,1,0:T(8,128)(2,1)} reshape(bf16[1,4,1,4,2,80,1536]{6,5,4,3,1,2,0:T(8,128)(2,1)} %get-tuple-element.148) | data formatting | bytes 15728640 | tf_op jit(solution)/shard_map/squeeze | solution.py:72
  585.0 9.3 %copy.17 = bf16[12,2560,128]{2,1,0:T(8,128)(2,1)} copy(bf16[12,2560,128]{2,0,1:T(8,128)(2,1)} %bitcast.67) | data formatting | bytes 15728640
  594.3 142.9 %while.11 = (s32[]{:T(128)}, bf16[12,640,128]{2,1,0:T(8,128)(2,1)S(1)}, pred[640]{0:T(1024)(128)(4,1)S(1)}, s32[12,3]{0,1:T(4,128)S(1)}, pred[1,2560]{1,0:T(4,12...) while((s32[]{:T(128)}, ...), condition=%wide.region_6.7_spmd.clone, body=%wide.region_4.6_spmd.clone.sunk | while | flops 866877440 | bytes 14808906 | solution.py:121
  595.0 8.9 %fusion.42 = (f32[640]{0:T(1024)S(1)}, f32[640,2560]{1,0:T(8,128)S(1)}) fusion(bf16[12,2560,128]{2,1,0:T(8,128)(2,1)} %get-tuple-element.290, s32[]{:T(128)} %get-tuple-element.268, bf16[12,640,128]{1,2,0:T(8,128)(2,1)} %get-tuple-element.289, pred[2560]{0:T(1024)(128)(4,1)S(1)} %reduce.4, s32[]{:T(128)} %bitcast.63, ...), kind=kOutput, calls=%fused_computation.69.clone.1 | convolution fusion | flops 444005760 | bytes 7418880 | tf_op jit(solution)/shard_map/while/body/eval_jaxpr/qd,kd->qk/dot_general | solution.py:112
  606.9 8.9 %fusion.42 = (f32[640]{0:T(1024)S(1)}, f32[640,2560]{1,0:T(8,128)S(1)}) fusion(bf16[12,2560,128]{2,1,0:T(8,128)(2,1)} %get-tuple-element.290, s32[]{:T(128)} %get-tuple-element.268, bf16[12,640,128]{1,2,0:T(8,128)(2,1)} %get-tuple-element.289, pred[2560]{0:T(1024)(128)(4,1)S(1)} %reduce.4, s32[]{:T(128)} %bitcast.63, ...), kind=kOutput, calls=%fused_computation.69.clone.1 | convolution fusion | flops 444005760 | bytes 7418880 | tf_op jit(solution)/shard_map/while/body/eval_jaxpr/qd,kd->qk/dot_general | solution.py:112
  618.8 8.9 %fusion.42 = (f32[640]{0:T(1024)S(1)}, f32[640,2560]{1,0:T(8,128)S(1)}) fusion(bf16[12,2560,128]{2,1,0:T(8,128)(2,1)} %get-tuple-element.290, s32[]{:T(128)} %get-tuple-element.268, bf16[12,640,128]{1,2,0:T(8,128)(2,1)} %get-tuple-element.289, pred[2560]{0:T(1024)(128)(4,1)S(1)} %reduce.4, s32[]{:T(128)} %bitcast.63, ...), kind=kOutput, calls=%fused_computation.69.clone.1 | convolution fusion | flops 444005760 | bytes 7418880 | tf_op jit(solution)/shard_map/while/body/eval_jaxpr/qd,kd->qk/dot_general | solution.py:112
  630.7 8.9 %fusion.42 = (f32[640]{0:T(1024)S(1)}, f32[640,2560]{1,0:T(8,128)S(1)}) fusion(bf16[12,2560,128]{2,1,0:T(8,128)(2,1)} %get-tuple-element.290, s32[]{:T(128)} %get-tuple-element.268, bf16[12,640,128]{1,2,0:T(8,128)(2,1)} %get-tuple-element.289, pred[2560]{0:T(1024)(128)(4,1)S(1)} %reduce.4, s32[]{:T(128)} %bitcast.63, ...), kind=kOutput, calls=%fused_computation.69.clone.1 | convolution fusion | flops 444005760 | bytes 7418880 | tf_op jit(solution)/shard_map/while/body/eval_jaxpr/qd,kd->qk/dot_general | solution.py:112
  642.6 8.9 %fusion.42 = (f32[640]{0:T(1024)S(1)}, f32[640,2560]{1,0:T(8,128)S(1)}) fusion(bf16[12,2560,128]{2,1,0:T(8,128)(2,1)} %get-tuple-element.290, s32[]{:T(128)} %get-tuple-element.268, bf16[12,640,128]{1,2,0:T(8,128)(2,1)} %get-tuple-element.289, pred[2560]{0:T(1024)(128)(4,1)S(1)} %reduce.4, s32[]{:T(128)} %bitcast.63, ...), kind=kOutput, calls=%fused_computation.69.clone.1 | convolution fusion | flops 444005760 | bytes 7418880 | tf_op jit(solution)/shard_map/while/body/eval_jaxpr/qd,kd->qk/dot_general | solution.py:112
  654.5 8.9 %fusion.42 = (f32[640]{0:T(1024)S(1)}, f32[640,2560]{1,0:T(8,128)S(1)}) fusion(bf16[12,2560,128]{2,1,0:T(8,128)(2,1)} %get-tuple-element.290, s32[]{:T(128)} %get-tuple-element.268, bf16[12,640,128]{1,2,0:T(8,128)(2,1)} %get-tuple-element.289, pred[2560]{0:T(1024)(128)(4,1)S(1)} %reduce.4, s32[]{:T(128)} %bitcast.63, ...), kind=kOutput, calls=%fused_computation.69.clone.1 | convolution fusion | flops 444005760 | bytes 7418880 | tf_op jit(solution)/shard_map/while/body/eval_jaxpr/qd,kd->qk/dot_general | solution.py:112
  666.5 8.9 %fusion.42 = (f32[640]{0:T(1024)S(1)}, f32[640,2560]{1,0:T(8,128)S(1)}) fusion(bf16[12,2560,128]{2,1,0:T(8,128)(2,1)} %get-tuple-element.290, s32[]{:T(128)} %get-tuple-element.268, bf16[12,640,128]{1,2,0:T(8,128)(2,1)} %get-tuple-element.289, pred[2560]{0:T(1024)(128)(4,1)S(1)} %reduce.4, s32[]{:T(128)} %bitcast.63, ...), kind=kOutput, calls=%fused_computation.69.clone.1 | convolution fusion | flops 444005760 | bytes 7418880 | tf_op jit(solution)/shard_map/while/body/eval_jaxpr/qd,kd->qk/dot_general | solution.py:112
  678.4 8.9 %fusion.42 = (f32[640]{0:T(1024)S(1)}, f32[640,2560]{1,0:T(8,128)S(1)}) fusion(bf16[12,2560,128]{2,1,0:T(8,128)(2,1)} %get-tuple-element.290, s32[]{:T(128)} %get-tuple-element.268, bf16[12,640,128]{1,2,0:T(8,128)(2,1)} %get-tuple-element.289, pred[2560]{0:T(1024)(128)(4,1)S(1)} %reduce.4, s32[]{:T(128)} %bitcast.63, ...), kind=kOutput, calls=%fused_computation.69.clone.1 | convolution fusion | flops 444005760 | bytes 7418880 | tf_op jit(solution)/shard_map/while/body/eval_jaxpr/qd,kd->qk/dot_general | solution.py:112
  690.3 8.9 %fusion.42 = (f32[640]{0:T(1024)S(1)}, f32[640,2560]{1,0:T(8,128)S(1)}) fusion(bf16[12,2560,128]{2,1,0:T(8,128)(2,1)} %get-tuple-element.290, s32[]{:T(128)} %get-tuple-element.268, bf16[12,640,128]{1,2,0:T(8,128)(2,1)} %get-tuple-element.289, pred[2560]{0:T(1024)(128)(4,1)S(1)} %reduce.4, s32[]{:T(128)} %bitcast.63, ...), kind=kOutput, calls=%fused_computation.69.clone.1 | convolution fusion | flops 444005760 | bytes 7418880 | tf_op jit(solution)/shard_map/while/body/eval_jaxpr/qd,kd->qk/dot_general | solution.py:112
  702.2 8.9 %fusion.42 = (f32[640]{0:T(1024)S(1)}, f32[640,2560]{1,0:T(8,128)S(1)}) fusion(bf16[12,2560,128]{2,1,0:T(8,128)(2,1)} %get-tuple-element.290, s32[]{:T(128)} %get-tuple-element.268, bf16[12,640,128]{1,2,0:T(8,128)(2,1)} %get-tuple-element.289, pred[2560]{0:T(1024)(128)(4,1)S(1)} %reduce.4, s32[]{:T(128)} %bitcast.63, ...), kind=kOutput, calls=%fused_computation.69.clone.1 | convolution fusion | flops 444005760 | bytes 7418880 | tf_op jit(solution)/shard_map/while/body/eval_jaxpr/qd,kd->qk/dot_general | solution.py:112
  714.1 8.9 %fusion.42 = (f32[640]{0:T(1024)S(1)}, f32[640,2560]{1,0:T(8,128)S(1)}) fusion(bf16[12,2560,128]{2,1,0:T(8,128)(2,1)} %get-tuple-element.290, s32[]{:T(128)} %get-tuple-element.268, bf16[12,640,128]{1,2,0:T(8,128)(2,1)} %get-tuple-element.289, pred[2560]{0:T(1024)(128)(4,1)S(1)} %reduce.4, s32[]{:T(128)} %bitcast.63, ...), kind=kOutput, calls=%fused_computation.69.clone.1 | convolution fusion | flops 444005760 | bytes 7418880 | tf_op jit(solution)/shard_map/while/body/eval_jaxpr/qd,kd->qk/dot_general | solution.py:112
  726.0 8.9 %fusion.42 = (f32[640]{0:T(1024)S(1)}, f32[640,2560]{1,0:T(8,128)S(1)}) fusion(bf16[12,2560,128]{2,1,0:T(8,128)(2,1)} %get-tuple-element.290, s32[]{:T(128)} %get-tuple-element.268, bf16[12,640,128]{1,2,0:T(8,128)(2,1)} %get-tuple-element.289, pred[2560]{0:T(1024)(128)(4,1)S(1)} %reduce.4, s32[]{:T(128)} %bitcast.63, ...), kind=kOutput, calls=%fused_computation.69.clone.1 | convolution fusion | flops 444005760 | bytes 7418880 | tf_op jit(solution)/shard_map/while/body/eval_jaxpr/qd,kd->qk/dot_general | solution.py:112
  (148 shorter events, 116.7 us)
Async XLA Ops:
  6.5 7.0 copy-start
  6.5 346.1 %all-gather.2.cloned.1.call-start = ((), (), s32[]{:S(2)}) async-start(), calls=%async_computation | async-start | bytes 28532736 | tf_op jit(solution)/shard_map/all_gather | solution.py:58
  7.3 6.3 copy-start.13
  7.3 6.3 copy-start.14
  403.5 31.7 %copy-start.3 = (bf16[1,2,1,2,2,80,1536]{6,5,4,3,1,2,0:T(8,128)(2,1)}, bf16[1,2,1,2,2,80,1536]{6,5,4,3,1,2,0:T(8,128)(2,1)S(1)}, u32[]{:S(2)}) copy-start(bf16[1,2,1,2,2,80,1536]{6,5,4,3,1,2,0:T(8,128)(2,1)S(1)} %multiply_convert_fusion) | copy-start | bytes 5898244
  403.9 29.6 %collective-permute-start = (bf16[2,1,1,2,2,80,1536]{6,5,4,3,1,2,0:T(8,128)(2,1)S(1)}, bf16[2,1,1,2,2,80,1536]{6,5,4,3,1,2,0:T(8,128)(2,1)S(1)}, u32[]{:S(2)}, u32[]{:S(2)}) collective-permute-start(bf16[2,1,1,2,2,80,1536]{6,5,4,3,1,2,0:T(8,128)(2,1)S(1)} %get-tuple-element.155), channel_id=1, source_target_pairs={{0,8},{8,16},{16,24},{24,32},{32,40},{40,48},{48,56},{56,64},{64,7... | collective-permute-start | bytes 5898248 | tf_op jit(solution)/shard_map/ppermute | solution.py:22
  406.8 28.5 %collective-permute-start.1 = (bf16[2,1,1,2,2,80,1536]{6,5,4,3,1,2,0:T(8,128)(2,1)S(1)}, bf16[2,1,1,2,2,80,1536]{6,5,4,3,1,2,0:T(8,128)(2,1)S(1)}, u32[]{:S(2)}, u32[]{:S(2)}) collective-permute-start(bf16[2,1,1,2,2,80,1536]{6,5,4,3,1,2,0:T(8,128)(2,1)S(1)} %get-tuple-element.156), channel_id=1, source_target_pairs={{8,0},{16,8},{24,16},{32,24},{40,32},{48,40},{56,48},{64,56},{72,6... | collective-permute-start | bytes 5898248 | tf_op jit(solution)/shard_map/ppermute | solution.py:24
  433.5 1.8 copy-start.5
  435.3 1.3 copy-start.7
  437.6 10.7 %copy-start.11 = (s32[32,32,80]{2,1,0:T(8,128)S(1)}, s32[32,32,80]{2,1,0:T(8,128)}, u32[]{:S(2)}) copy-start(s32[32,32,80]{2,1,0:T(8,128)} %param.17) | copy-start | bytes 983044
  441.1 86.4 %collective-permute-start.2 = (bf16[2,4,1,1,2,80,1536]{6,5,4,3,1,2,0:T(8,128)(2,1)}, bf16[2,4,1,1,2,80,1536]{6,5,4,3,1,2,0:T(8,128)(2,1)}, u32[]{:S(2)}, u32[]{:S(2)}) collective-permute-start(bf16[2,4,1,1,2,80,1536]{6,5,4,3,1,2,0:T(8,128)(2,1)} %get-tuple-element.153), channel_id=1, source_target_pairs={{0,1},{1,2},{2,3},{3,4},{4,5},{5,6},{6,7},{8,9},{9,10},{10,11},{11... | collective-permute-start | bytes 11796488 | tf_op jit(solution)/shard_map/ppermute | solution.py:22
  446.8 86.6 %collective-permute-start.3 = (bf16[2,4,1,1,2,80,1536]{6,5,4,3,1,2,0:T(8,128)(2,1)}, bf16[2,4,1,1,2,80,1536]{6,5,4,3,1,2,0:T(8,128)(2,1)}, u32[]{:S(2)}, u32[]{:S(2)}) collective-permute-start(bf16[2,4,1,1,2,80,1536]{6,5,4,3,1,2,0:T(8,128)(2,1)} %get-tuple-element.154), channel_id=1, source_target_pairs={{1,0},{2,1},{3,2},{4,3},{5,4},{6,5},{7,6},{9,8},{10,9},{11,10},{12... | collective-permute-start | bytes 11796488 | tf_op jit(solution)/shard_map/ppermute | solution.py:24
  454.9 3.3 copy-start.2
  454.9 3.3 copy-start.15
  457.5 76.0 %copy-start.4 = (bf16[1,2,1,2,2,80,1536]{6,5,4,3,1,2,0:T(8,128)(2,1)S(1)}, bf16[1,2,1,2,2,80,1536]{6,5,4,3,1,2,0:T(8,128)(2,1)}, u32[]{:S(2)}) copy-start(bf16[1,2,1,2,2,80,1536]{6,5,4,3,1,2,0:T(8,128)(2,1)} %copy-done.3) | copy-start | bytes 5898244
  457.5 76.0 %copy-start.6 = (bf16[2,1,1,2,2,80,1536]{6,5,4,3,1,2,0:T(8,128)(2,1)S(1)}, bf16[2,1,1,2,2,80,1536]{6,5,4,3,1,2,0:T(8,128)(2,1)}, u32[]{:S(2)}) copy-start(bf16[2,1,1,2,2,80,1536]{6,5,4,3,1,2,0:T(8,128)(2,1)} %copy-done.5) | copy-start | bytes 5898244
  457.5 76.0 %copy-start.8 = (bf16[2,1,1,2,2,80,1536]{6,5,4,3,1,2,0:T(8,128)(2,1)S(1)}, bf16[2,1,1,2,2,80,1536]{6,5,4,3,1,2,0:T(8,128)(2,1)}, u32[]{:S(2)}) copy-start(bf16[2,1,1,2,2,80,1536]{6,5,4,3,1,2,0:T(8,128)(2,1)} %copy-done.7) | copy-start | bytes 5898244
  585.0 9.3 %copy-start.9 = (bf16[12,640,128]{2,1,0:T(8,128)(2,1)S(1)}, bf16[12,640,128]{2,1,0:T(8,128)(2,1)}, u32[]{:S(2)}) copy-start(bf16[12,640,128]{2,1,0:T(8,128)(2,1)} %custom-call) | copy-start | bytes 5898244
  585.0 9.3 %copy-start.12 = (s32[12,3]{0,1:T(4,128)S(1)}, s32[12,3]{0,1:T(4,128)}, u32[]{:S(2)}) copy-start(s32[12,3]{0,1:T(4,128)} %param.16) | copy-start | bytes 436
  737.2 1.3 copy-start.10
  738.5 5.5 copy-start.1
Sparse Core Ops, SparseCore 0:
  9.1 343.5 all-gather.1
where the time goes:
time: 753 us; the launch traced here: 751 us
  waiting for transfers between devices  430 us (57%)
  matrix products  158 us (21%)
  local copies, waits for them, and re-layouts  96.6 us (13%)
  other arithmetic  35.8 us (5%)
  starting transfers between devices  16.4 us (2%)
  between operations  13.7 us (2%)
    all_gather x1, waiting for transfers between devices, per_device(): full_weight = lax.all_gather(w_qkv, ('tm', 'height'), axis=0, tiled=True)  334 us
    dot_general x12, matrix products, per_head(): jnp.einsum('qd,kd->qk', query_one, key_one, preferred_element_type=jnp.fl...  107 us
    ppermute x2, waiting for transfers between devices, with_halo(): lax.ppermute(tail, axis, [(i, (i + 1) % count) for i in range(ends)])  87.7 us
    dot_general x12, matrix products, per_head(): result = jnp.dot(weights, value_one, preferred_element_type=jnp.float32)  26.8 us
    dot_general x1, matrix products, per_device(): qkv = jnp.dot(modulated, full_weight, preferred_element_type=jnp.float32)  23.6 us
    unnamed x34, local copies, waits for them, and re-layouts  21.7 us
    squeeze x1, local copies, waits for them, and re-layouts, per_device(): key_heads = jnp.transpose(extended[0], (1, 0, 2))  15.1 us
    squeeze x1, local copies, waits for them, and re-layouts, per_device(): value_heads = jnp.transpose(extended[1], (1, 0, 2))  15.1 us
  transfers between devices with their start and end apart: 5, of which 5 were waited for; matrix products, arithmetic and copies ran while one was open for 3% of the time, Pallas kernels for 0%

commit v1 on v0

--- a/solution.py
+++ b/solution.py
@@ -9,6 +9,13 @@
 TH = 2
 TW = 8
 EPS = 1e-06
+
+
+def swapped_in(x, name, along):
+    n_dev = lax.axis_size(name)
+    parts = jnp.stack([x for _ in range(n_dev)])
+    parts = lax.all_to_all(parts, name, split_axis=0, concat_axis=0)
+    return jnp.concatenate(parts, axis=along)
 
 
 def with_halo(cells, sides, width):
@@ -55,7 +62,7 @@
     frame_count, row_count, width, features = tokens.shape
     token_count = frame_count * row_count * width
     modulated = modulate(tokens.reshape(token_count, features), mod_scale, mod_shift)
-    full_weight = lax.all_gather(w_qkv, ("tm", "height"), axis=0, tiled=True)
+    full_weight = swapped_in(w_qkv, ("tm", "height"), 0)
     qkv = jnp.dot(modulated, full_weight, preferred_element_type=jnp.float32)
     inner = qkv.shape[1] // 3
     query = head_norm(qkv[:, :inner].reshape(token_count, HEADS, HDIM), q_gain)

time: 753 us -> 847 us (1.12)
  waiting for transfers between devices: 430 us -> 495 us
  starting transfers between devices: 16.4 us -> 47.2 us
  between operations: 13.7 us -> 0.34 us
  local copies, waits for them, and re-layouts: 96.6 us -> 107 us
    all_to_all x0 -> x1, waiting for transfers between devices: none -> 415 us  [swapped_in(): parts = lax.all_to_all(parts, name, split_axis=0, concat_axis=0)]
    all_gather x1 -> x0, waiting for transfers between devices: 334 us -> none  [per_device(): full_weight = lax.all_gather(w_qkv, ('tm', 'height'), axis=0, tiled=True)]
    ppermute x2, starting transfers between devices: 8.63 us -> 26.6 us  [with_halo(): lax.ppermute(tail, axis, [(i, (i + 1) % count) for i in range(ends)])]
    ppermute x2, waiting for transfers between devices: 87.7 us -> 71.4 us  [with_halo(): lax.ppermute(tail, axis, [(i, (i + 1) % count) for i in range(ends)])]
    all_to_all x0 -> x1, starting transfers between devices: none -> 10.9 us  [swapped_in(): parts = lax.all_to_all(parts, name, split_axis=0, concat_axis=0)]
    another operation x0 -> x1, local copies, waits for them, and re-layouts: none -> 10.3 us  [swapped_in(): parts = jnp.stack([x for _ in range(n_dev)])]
    unnamed x34 -> x36, local copies, waits for them, and re-layouts: 21.7 us -> 22.2 us
  transfers between devices with their start and end apart: 5 -> 5, of which waited for: 5 -> 5; matrix products, arithmetic and copies ran while one was open for 3% -> 2% of each run, Pallas kernels for 0% -> 0%
where the time goes in v1:
time: 847 us; the launch traced here: 839 us
  waiting for transfers between devices  495 us (58%)
  matrix products  157 us (19%)
  local copies, waits for them, and re-layouts  107 us (13%)
  starting transfers between devices  47.2 us (6%)
  other arithmetic  32.4 us (4%)
    all_to_all x1, waiting for transfers between devices, swapped_in(): parts = lax.all_to_all(parts, name, split_axis=0, concat_axis=0)  415 us
    dot_general x12, matrix products, per_head(): jnp.einsum('qd,kd->qk', query_one, key_one, preferred_element_type=jnp.fl...  107 us
    ppermute x2, waiting for transfers between devices, with_halo(): lax.ppermute(tail, axis, [(i, (i + 1) % count) for i in range(ends)])  71.4 us
    dot_general x12, matrix products, per_head(): result = jnp.dot(weights, value_one, preferred_element_type=jnp.float32)  26.7 us
    ppermute x2, starting transfers between devices, with_halo(): lax.ppermute(tail, axis, [(i, (i + 1) % count) for i in range(ends)])  26.6 us
    dot_general x1, matrix products, per_device(): qkv = jnp.dot(modulated, full_weight, preferred_element_type=jnp.float32)  23.6 us
    unnamed x36, local copies, waits for them, and re-layouts  22.2 us
  transfers between devices with their start and end apart: 5, of which 5 were waited for; matrix products, arithmetic and copies ran while one was open for 2% of the time, Pallas kernels for 0%

profile of v1, /device:TPU:4, one launch (start us, length us, event | category | flops | bytes accessed | tf_op | source)
XLA Modules:
  0.0 839.2 jit_solution(18426470937499192064)
XLA Ops:
  0.0 10.3 %stack.4 = bf16[128,24,4608]{2,1,0:T(8,128)(2,1)} broadcast(bf16[24,4608]{1,0:T(8,128)(2,1)} %param.13), dimensions={1,2} | broadcast | bytes 28532736 | tf_op jit(solution)/shard_map/stack | solution.py:16
  10.3 10.9 %all-to-all-start = ((bf16[128,24,4608]{2,1,0:T(8,128)(2,1)}), bf16[128,24,4608]{2,1,0:T(8,128)(2,1)}, u32[]{:S(2)}, u32[]{:S(2)}) async-start(bf16[128,24,4608]{2,1,0:T(8,128)(2,1)} %stack.4), calls=%async_computation | async-start | bytes 56623104 | tf_op jit(solution)/shard_map/all_to_all | solution.py:17
  29.1 415.0 %all-to-all-done = bf16[128,24,4608]{2,1,0:T(8,128)(2,1)} async-done(((bf16[128,24,4608]{2,1,0:T(8,128)(2,1)}), bf16[128,24,4608]{2,1,0:T(8,128)(2,1)}, u32[]{:S(2)}, u32[]{:S(2)}) %all-to-all-start) | async-done | bytes 28311584 | tf_op jit(solution)/shard_map/all_to_all | solution.py:17
  444.1 23.6 %fusion.35 = f32[640,4608]{1,0:T(8,128)S(1)} fusion(bf16[640,3072]{1,0:T(8,128)(2,1)} %bitcast.67, bf16[3072,4608]{1,0:T(8,128)(2,1)} %bitcast.1), kind=kOutput, calls=%fused_computation.73 | convolution fusion | flops 18119393280 | bytes 44040192 | tf_op jit(solution)/shard_map/dot_general | solution.py:66
  511.3 20.2 %collective-permute-done = bf16[2,1,1,2,2,80,1536]{6,5,4,3,1,2,0:T(8,128)(2,1)S(1)} collective-permute-done((bf16[2,1,1,2,2,80,1536]{6,5,4,3,1,2,0:T(8,128)(2,1)S(1)}, bf16[2,1,1,2,2,80,1536]{6,5,4,3,1,2,0:T(8,128)(2,1)S(1)}, u32[]{:S(2)}, u32[]{:S(2)}) %collective-permute-start) | collective-permute-done | bytes 1966112 | tf_op jit(solution)/shard_map/ppermute | solution.py:29
  539.1 19.1 %collective-permute-start.2 = (bf16[2,4,1,1,2,80,1536]{6,5,4,3,1,2,0:T(8,128)(2,1)}, bf16[2,4,1,1,2,80,1536]{6,5,4,3,1,2,0:T(8,128)(2,1)}, u32[]{:S(2)}, u32[]{:S(2)}) collective-permute-start(bf16[2,4,1,1,2,80,1536]{6,5,4,3,1,2,0:T(8,128)(2,1)} %get-tuple-element.153), channel_id=1, source_target_pairs={{0,1},{1,2},{2,3},{3,4},{4,5},{5,6},{6,7},{8,9},{9,10},{10,11},{11... | collective-permute-start | bytes 11796488 | tf_op jit(solution)/shard_map/ppermute | solution.py:29
  571.2 51.2 %collective-permute-done.2 = bf16[2,4,1,1,2,80,1536]{6,5,4,3,1,2,0:T(8,128)(2,1)} collective-permute-done((bf16[2,4,1,1,2,80,1536]{6,5,4,3,1,2,0:T(8,128)(2,1)}, bf16[2,4,1,1,2,80,1536]{6,5,4,3,1,2,0:T(8,128)(2,1)}, u32[]{:S(2)}, u32[]{:S(2)}) %collective-permute-start.2) | collective-permute-done | bytes 3932192 | tf_op jit(solution)/shard_map/ppermute | solution.py:29
  641.4 15.1 %squeeze.28 = bf16[2560,12,128]{2,1,0:T(8,128)(2,1)} reshape(bf16[1,4,1,4,2,80,1536]{6,5,4,3,1,2,0:T(8,128)(2,1)} %get-tuple-element.149) | data formatting | bytes 15728640 | tf_op jit(solution)/shard_map/squeeze | solution.py:78
  656.5 9.1 %copy.16 = bf16[12,2560,128]{2,1,0:T(8,128)(2,1)} copy(bf16[12,2560,128]{2,0,1:T(8,128)(2,1)} %bitcast.58) | data formatting | bytes 15728640
  665.7 15.1 %squeeze.29 = bf16[2560,12,128]{2,1,0:T(8,128)(2,1)} reshape(bf16[1,4,1,4,2,80,1536]{6,5,4,3,1,2,0:T(8,128)(2,1)} %get-tuple-element.148) | data formatting | bytes 15728640 | tf_op jit(solution)/shard_map/squeeze | solution.py:79
  680.8 9.3 %copy.17 = bf16[12,2560,128]{2,1,0:T(8,128)(2,1)} copy(bf16[12,2560,128]{2,0,1:T(8,128)(2,1)} %bitcast.59) | data formatting | bytes 15728640
  690.1 142.3 %while.11 = (s32[]{:T(128)}, bf16[12,640,128]{2,1,0:T(8,128)(2,1)S(1)}, pred[640]{0:T(1024)(128)(4,1)S(1)}, s32[12,3]{0,1:T(4,128)S(1)}, pred[1,2560]{1,0:T(4,12...) while((s32[]{:T(128)}, ...), condition=%wide.region_6.7_spmd.clone, body=%wide.region_4.6_spmd.clone.sunk | while | flops 866877440 | bytes 14808906 | solution.py:128
  690.8 8.9 %fusion.44 = (f32[640]{0:T(1024)S(1)}, f32[640,2560]{1,0:T(8,128)S(1)}) fusion(bf16[12,2560,128]{2,1,0:T(8,128)(2,1)} %get-tuple-element.290, s32[]{:T(128)} %get-tuple-element.268, bf16[12,640,128]{1,2,0:T(8,128)(2,1)} %get-tuple-element.289, pred[2560]{0:T(1024)(128)(4,1)S(1)} %reduce.4, s32[]{:T(128)} %bitcast.55, ...), kind=kOutput, calls=%fused_computation.70.clone.1 | convolution fusion | flops 444005760 | bytes 7418880 | tf_op jit(solution)/shard_map/while/body/eval_jaxpr/qd,kd->qk/dot_general | solution.py:119
  702.6 8.9 %fusion.44 = (f32[640]{0:T(1024)S(1)}, f32[640,2560]{1,0:T(8,128)S(1)}) fusion(bf16[12,2560,128]{2,1,0:T(8,128)(2,1)} %get-tuple-element.290, s32[]{:T(128)} %get-tuple-element.268, bf16[12,640,128]{1,2,0:T(8,128)(2,1)} %get-tuple-element.289, pred[2560]{0:T(1024)(128)(4,1)S(1)} %reduce.4, s32[]{:T(128)} %bitcast.55, ...), kind=kOutput, calls=%fused_computation.70.clone.1 | convolution fusion | flops 444005760 | bytes 7418880 | tf_op jit(solution)/shard_map/while/body/eval_jaxpr/qd,kd->qk/dot_general | solution.py:119
  714.5 8.9 %fusion.44 = (f32[640]{0:T(1024)S(1)}, f32[640,2560]{1,0:T(8,128)S(1)}) fusion(bf16[12,2560,128]{2,1,0:T(8,128)(2,1)} %get-tuple-element.290, s32[]{:T(128)} %get-tuple-element.268, bf16[12,640,128]{1,2,0:T(8,128)(2,1)} %get-tuple-element.289, pred[2560]{0:T(1024)(128)(4,1)S(1)} %reduce.4, s32[]{:T(128)} %bitcast.55, ...), kind=kOutput, calls=%fused_computation.70.clone.1 | convolution fusion | flops 444005760 | bytes 7418880 | tf_op jit(solution)/shard_map/while/body/eval_jaxpr/qd,kd->qk/dot_general | solution.py:119
  726.3 8.9 %fusion.44 = (f32[640]{0:T(1024)S(1)}, f32[640,2560]{1,0:T(8,128)S(1)}) fusion(bf16[12,2560,128]{2,1,0:T(8,128)(2,1)} %get-tuple-element.290, s32[]{:T(128)} %get-tuple-element.268, bf16[12,640,128]{1,2,0:T(8,128)(2,1)} %get-tuple-element.289, pred[2560]{0:T(1024)(128)(4,1)S(1)} %reduce.4, s32[]{:T(128)} %bitcast.55, ...), kind=kOutput, calls=%fused_computation.70.clone.1 | convolution fusion | flops 444005760 | bytes 7418880 | tf_op jit(solution)/shard_map/while/body/eval_jaxpr/qd,kd->qk/dot_general | solution.py:119
  738.2 8.9 %fusion.44 = (f32[640]{0:T(1024)S(1)}, f32[640,2560]{1,0:T(8,128)S(1)}) fusion(bf16[12,2560,128]{2,1,0:T(8,128)(2,1)} %get-tuple-element.290, s32[]{:T(128)} %get-tuple-element.268, bf16[12,640,128]{1,2,0:T(8,128)(2,1)} %get-tuple-element.289, pred[2560]{0:T(1024)(128)(4,1)S(1)} %reduce.4, s32[]{:T(128)} %bitcast.55, ...), kind=kOutput, calls=%fused_computation.70.clone.1 | convolution fusion | flops 444005760 | bytes 7418880 | tf_op jit(solution)/shard_map/while/body/eval_jaxpr/qd,kd->qk/dot_general | solution.py:119
  750.1 8.9 %fusion.44 = (f32[640]{0:T(1024)S(1)}, f32[640,2560]{1,0:T(8,128)S(1)}) fusion(bf16[12,2560,128]{2,1,0:T(8,128)(2,1)} %get-tuple-element.290, s32[]{:T(128)} %get-tuple-element.268, bf16[12,640,128]{1,2,0:T(8,128)(2,1)} %get-tuple-element.289, pred[2560]{0:T(1024)(128)(4,1)S(1)} %reduce.4, s32[]{:T(128)} %bitcast.55, ...), kind=kOutput, calls=%fused_computation.70.clone.1 | convolution fusion | flops 444005760 | bytes 7418880 | tf_op jit(solution)/shard_map/while/body/eval_jaxpr/qd,kd->qk/dot_general | solution.py:119
  761.9 8.9 %fusion.44 = (f32[640]{0:T(1024)S(1)}, f32[640,2560]{1,0:T(8,128)S(1)}) fusion(bf16[12,2560,128]{2,1,0:T(8,128)(2,1)} %get-tuple-element.290, s32[]{:T(128)} %get-tuple-element.268, bf16[12,640,128]{1,2,0:T(8,128)(2,1)} %get-tuple-element.289, pred[2560]{0:T(1024)(128)(4,1)S(1)} %reduce.4, s32[]{:T(128)} %bitcast.55, ...), kind=kOutput, calls=%fused_computation.70.clone.1 | convolution fusion | flops 444005760 | bytes 7418880 | tf_op jit(solution)/shard_map/while/body/eval_jaxpr/qd,kd->qk/dot_general | solution.py:119
  773.8 8.9 %fusion.44 = (f32[640]{0:T(1024)S(1)}, f32[640,2560]{1,0:T(8,128)S(1)}) fusion(bf16[12,2560,128]{2,1,0:T(8,128)(2,1)} %get-tuple-element.290, s32[]{:T(128)} %get-tuple-element.268, bf16[12,640,128]{1,2,0:T(8,128)(2,1)} %get-tuple-element.289, pred[2560]{0:T(1024)(128)(4,1)S(1)} %reduce.4, s32[]{:T(128)} %bitcast.55, ...), kind=kOutput, calls=%fused_computation.70.clone.1 | convolution fusion | flops 444005760 | bytes 7418880 | tf_op jit(solution)/shard_map/while/body/eval_jaxpr/qd,kd->qk/dot_general | solution.py:119
  785.6 8.9 %fusion.44 = (f32[640]{0:T(1024)S(1)}, f32[640,2560]{1,0:T(8,128)S(1)}) fusion(bf16[12,2560,128]{2,1,0:T(8,128)(2,1)} %get-tuple-element.290, s32[]{:T(128)} %get-tuple-element.268, bf16[12,640,128]{1,2,0:T(8,128)(2,1)} %get-tuple-element.289, pred[2560]{0:T(1024)(128)(4,1)S(1)} %reduce.4, s32[]{:T(128)} %bitcast.55, ...), kind=kOutput, calls=%fused_computation.70.clone.1 | convolution fusion | flops 444005760 | bytes 7418880 | tf_op jit(solution)/shard_map/while/body/eval_jaxpr/qd,kd->qk/dot_general | solution.py:119
  797.5 8.9 %fusion.44 = (f32[640]{0:T(1024)S(1)}, f32[640,2560]{1,0:T(8,128)S(1)}) fusion(bf16[12,2560,128]{2,1,0:T(8,128)(2,1)} %get-tuple-element.290, s32[]{:T(128)} %get-tuple-element.268, bf16[12,640,128]{1,2,0:T(8,128)(2,1)} %get-tuple-element.289, pred[2560]{0:T(1024)(128)(4,1)S(1)} %reduce.4, s32[]{:T(128)} %bitcast.55, ...), kind=kOutput, calls=%fused_computation.70.clone.1 | convolution fusion | flops 444005760 | bytes 7418880 | tf_op jit(solution)/shard_map/while/body/eval_jaxpr/qd,kd->qk/dot_general | solution.py:119
  809.3 8.9 %fusion.44 = (f32[640]{0:T(1024)S(1)}, f32[640,2560]{1,0:T(8,128)S(1)}) fusion(bf16[12,2560,128]{2,1,0:T(8,128)(2,1)} %get-tuple-element.290, s32[]{:T(128)} %get-tuple-element.268, bf16[12,640,128]{1,2,0:T(8,128)(2,1)} %get-tuple-element.289, pred[2560]{0:T(1024)(128)(4,1)S(1)} %reduce.4, s32[]{:T(128)} %bitcast.55, ...), kind=kOutput, calls=%fused_computation.70.clone.1 | convolution fusion | flops 444005760 | bytes 7418880 | tf_op jit(solution)/shard_map/while/body/eval_jaxpr/qd,kd->qk/dot_general | solution.py:119
  821.2 8.9 %fusion.44 = (f32[640]{0:T(1024)S(1)}, f32[640,2560]{1,0:T(8,128)S(1)}) fusion(bf16[12,2560,128]{2,1,0:T(8,128)(2,1)} %get-tuple-element.290, s32[]{:T(128)} %get-tuple-element.268, bf16[12,640,128]{1,2,0:T(8,128)(2,1)} %get-tuple-element.289, pred[2560]{0:T(1024)(128)(4,1)S(1)} %reduce.4, s32[]{:T(128)} %bitcast.55, ...), kind=kOutput, calls=%fused_computation.70.clone.1 | convolution fusion | flops 444005760 | bytes 7418880 | tf_op jit(solution)/shard_map/while/body/eval_jaxpr/qd,kd->qk/dot_general | solution.py:119
  (148 shorter events, 132.4 us)
Async XLA Ops:
  0.0 25.7 %copy-start = (f32[128]{0:T(128)S(1)}, f32[128]{0:T(128)}, u32[]{:S(2)}) copy-start(f32[128]{0:T(128)} %param.15) | copy-start | bytes 1540
  10.3 433.8 %all-to-all-start = ((bf16[128,24,4608]{2,1,0:T(8,128)(2,1)}), bf16[128,24,4608]{2,1,0:T(8,128)(2,1)}, u32[]{:S(2)}, u32[]{:S(2)}) async-start(bf16[128,24,4608]{2,1,0:T(8,128)(2,1)} %stack.4), calls=%async_computation | async-start | bytes 56623104 | tf_op jit(solution)/shard_map/all_to_all | solution.py:17
  21.2 3.3 copy-start.2
  21.2 4.5 copy-start.14
  21.2 4.5 copy-start.15
  495.0 38.2 %copy-start.4 = (bf16[1,2,1,2,2,80,1536]{6,5,4,3,1,2,0:T(8,128)(2,1)}, bf16[1,2,1,2,2,80,1536]{6,5,4,3,1,2,0:T(8,128)(2,1)S(1)}, u32[]{:S(2)}) copy-start(bf16[1,2,1,2,2,80,1536]{6,5,4,3,1,2,0:T(8,128)(2,1)S(1)} %multiply_convert_fusion) | copy-start | bytes 5898244
  495.4 36.1 %collective-permute-start = (bf16[2,1,1,2,2,80,1536]{6,5,4,3,1,2,0:T(8,128)(2,1)S(1)}, bf16[2,1,1,2,2,80,1536]{6,5,4,3,1,2,0:T(8,128)(2,1)S(1)}, u32[]{:S(2)}, u32[]{:S(2)}) collective-permute-start(bf16[2,1,1,2,2,80,1536]{6,5,4,3,1,2,0:T(8,128)(2,1)S(1)} %get-tuple-element.155), channel_id=1, source_target_pairs={{0,8},{8,16},{16,24},{24,32},{32,40},{40,48},{48,56},{56,64},{64,7... | collective-permute-start | bytes 5898248 | tf_op jit(solution)/shard_map/ppermute | solution.py:29
  502.9 30.4 %collective-permute-start.1 = (bf16[2,1,1,2,2,80,1536]{6,5,4,3,1,2,0:T(8,128)(2,1)S(1)}, bf16[2,1,1,2,2,80,1536]{6,5,4,3,1,2,0:T(8,128)(2,1)S(1)}, u32[]{:S(2)}, u32[]{:S(2)}) collective-permute-start(bf16[2,1,1,2,2,80,1536]{6,5,4,3,1,2,0:T(8,128)(2,1)S(1)} %get-tuple-element.156), channel_id=1, source_target_pairs={{8,0},{16,8},{24,16},{32,24},{40,32},{48,40},{56,48},{64,56},{72,6... | collective-permute-start | bytes 5898248 | tf_op jit(solution)/shard_map/ppermute | solution.py:31
  531.5 1.8 copy-start.6
  533.2 1.4 copy-start.8
  535.7 23.8 %copy-start.12 = (s32[32,32,80]{2,1,0:T(8,128)S(1)}, s32[32,32,80]{2,1,0:T(8,128)}, u32[]{:S(2)}) copy-start(s32[32,32,80]{2,1,0:T(8,128)} %param.17) | copy-start | bytes 983044
  539.1 83.4 %collective-permute-start.2 = (bf16[2,4,1,1,2,80,1536]{6,5,4,3,1,2,0:T(8,128)(2,1)}, bf16[2,4,1,1,2,80,1536]{6,5,4,3,1,2,0:T(8,128)(2,1)}, u32[]{:S(2)}, u32[]{:S(2)}) collective-permute-start(bf16[2,4,1,1,2,80,1536]{6,5,4,3,1,2,0:T(8,128)(2,1)} %get-tuple-element.153), channel_id=1, source_target_pairs={{0,1},{1,2},{2,3},{3,4},{4,5},{5,6},{6,7},{8,9},{9,10},{10,11},{11... | collective-permute-start | bytes 11796488 | tf_op jit(solution)/shard_map/ppermute | solution.py:29
  558.2 71.1 %collective-permute-start.3 = (bf16[2,4,1,1,2,80,1536]{6,5,4,3,1,2,0:T(8,128)(2,1)}, bf16[2,4,1,1,2,80,1536]{6,5,4,3,1,2,0:T(8,128)(2,1)}, u32[]{:S(2)}, u32[]{:S(2)}) collective-permute-start(bf16[2,4,1,1,2,80,1536]{6,5,4,3,1,2,0:T(8,128)(2,1)} %get-tuple-element.154), channel_id=1, source_target_pairs={{1,0},{2,1},{3,2},{4,3},{5,4},{6,5},{7,6},{9,8},{10,9},{11,10},{12... | collective-permute-start | bytes 11796488 | tf_op jit(solution)/shard_map/ppermute | solution.py:31
  566.0 3.3 copy-start.3
  566.0 3.3 copy-start.16
  568.6 60.6 %copy-start.5 = (bf16[1,2,1,2,2,80,1536]{6,5,4,3,1,2,0:T(8,128)(2,1)S(1)}, bf16[1,2,1,2,2,80,1536]{6,5,4,3,1,2,0:T(8,128)(2,1)}, u32[]{:S(2)}) copy-start(bf16[1,2,1,2,2,80,1536]{6,5,4,3,1,2,0:T(8,128)(2,1)} %copy-done.4) | copy-start | bytes 5898244
  568.6 60.6 %copy-start.7 = (bf16[2,1,1,2,2,80,1536]{6,5,4,3,1,2,0:T(8,128)(2,1)S(1)}, bf16[2,1,1,2,2,80,1536]{6,5,4,3,1,2,0:T(8,128)(2,1)}, u32[]{:S(2)}) copy-start(bf16[2,1,1,2,2,80,1536]{6,5,4,3,1,2,0:T(8,128)(2,1)} %copy-done.6) | copy-start | bytes 5898244
  568.6 60.6 %copy-start.9 = (bf16[2,1,1,2,2,80,1536]{6,5,4,3,1,2,0:T(8,128)(2,1)S(1)}, bf16[2,1,1,2,2,80,1536]{6,5,4,3,1,2,0:T(8,128)(2,1)}, u32[]{:S(2)}) copy-start(bf16[2,1,1,2,2,80,1536]{6,5,4,3,1,2,0:T(8,128)(2,1)} %copy-done.8) | copy-start | bytes 5898244
  680.8 9.3 %copy-start.10 = (bf16[12,640,128]{2,1,0:T(8,128)(2,1)S(1)}, bf16[12,640,128]{2,1,0:T(8,128)(2,1)}, u32[]{:S(2)}) copy-start(bf16[12,640,128]{2,1,0:T(8,128)(2,1)} %custom-call) | copy-start | bytes 5898244
  680.8 9.3 %copy-start.13 = (s32[12,3]{0,1:T(4,128)S(1)}, s32[12,3]{0,1:T(4,128)}, u32[]{:S(2)}) copy-start(s32[12,3]{0,1:T(4,128)} %param.16) | copy-start | bytes 436
  832.4 1.3 copy-start.11
  833.7 5.5 copy-start.1
